TPU v7x, 32 devices: a whole 2x2x4 slice. The times are simulated.
32 devices in a mesh: dp: 8 (over y, x, core), tensor: 4 (over z).
Axes of the slice: x: 2, y: 2, z: 4, core: 2. Of those that a mesh axis runs over, the one named last changes fastest.
Arguments:
- tokens: bfloat16 [8192, 768], P(('dp', 'tensor')), may hold values from -60 to 60
- encoder: bfloat16 [4096, 768], P(('dp', 'tensor')), may hold values from -6 to 6
- segments: int32 [8, 1024], P('dp'), may hold values from 0 to 5, never falling along the last dimension, each value on 1 to 800 neighbouring positions
- rel_bucket: int32 [1024], replicated, may hold values from 0 to 31
- out_grad: bfloat16 [8192, 768], P(('dp', 'tensor')), may hold values from -6 to 6
- self_q: bfloat16 [768, 768], P('dp', 'tensor'), may hold values from -0.109375 to 0.109375
- self_k: bfloat16 [768, 768], P('dp', 'tensor'), may hold values from -0.109375 to 0.109375
- self_v: bfloat16 [768, 768], P('dp', 'tensor'), may hold values from -0.21875 to 0.21875
- self_o: bfloat16 [768, 768], P('tensor', 'dp'), may hold values from -0.875 to 0.875
- cross_q: bfloat16 [768, 768], P('dp', 'tensor'), may hold values from -0.109375 to 0.109375
- cross_k: bfloat16 [768, 768], P('dp', 'tensor'), may hold values from -0.109375 to 0.109375
- cross_v: bfloat16 [768, 768], P('dp', 'tensor'), may hold values from -0.21875 to 0.21875
- cross_o: bfloat16 [768, 768], P('tensor', 'dp'), may hold values from -0.875 to 0.875
- ffn_gate: bfloat16 [768, 2048], P('dp', 'tensor'), may hold values from -0.21875 to 0.21875
- ffn_up: bfloat16 [768, 2048], P('dp', 'tensor'), may hold values from -0.21875 to 0.21875
- ffn_down: bfloat16 [2048, 768], P('tensor', 'dp'), may hold values from -0.125 to 0.125
- bias_table: bfloat16 [32, 12], P(None, 'tensor'), may hold values from -3 to 3
- norm_gains: bfloat16 [3, 768], P(None, 'dp'), may hold values from 0.5 to 1.5
Outputs:
- layer_out: bfloat16 [8192, 768], P(('dp', 'tensor'))
- tokens_grad: float32 [8192, 768], P(('dp', 'tensor'))
- encoder_grad: float32 [4096, 768], P(('dp', 'tensor'))
- self_q_grad: float32 [768, 768], P('dp', 'tensor')
- self_k_grad: float32 [768, 768], P('dp', 'tensor')
- self_v_grad: float32 [768, 768], P('dp', 'tensor')
- self_o_grad: float32 [768, 768], P('tensor', 'dp')
- cross_q_grad: float32 [768, 768], P('dp', 'tensor')
- cross_k_grad: float32 [768, 768], P('dp', 'tensor')
- cross_v_grad: float32 [768, 768], P('dp', 'tensor')
- cross_o_grad: float32 [768, 768], P('tensor', 'dp')
- ffn_gate_grad: float32 [768, 2048], P('dp', 'tensor')
- ffn_up_grad: float32 [768, 2048], P('dp', 'tensor')
- ffn_down_grad: float32 [2048, 768], P('tensor', 'dp')
- bias_table_grad: float32 [32, 12], P(None, 'tensor')
- norm_gains_grad: float32 [3, 768], P(None, 'dp')
Inputs may be any that keep to these rules, and one draw needn't show every extreme that they name: `segments`: within each sequence the numbers never fall; every document holds at most 800 tokens and some holds exactly 800.
All inputs are finite; a program needn't handle non-finite values.
Results may differ from a plain program's by a relative error of at most 0.04.
Values may be sent and summed in bfloat16 or wider, within the bound.
A program may use at most 192 MiB of HBM per device.

v0:
```python
from functools import partial

import jax
import jax.numpy as jnp
from jax import lax
from jax.experimental import pallas as pl
from jax.experimental.pallas import tpu as pltpu
from jax.sharding import PartitionSpec as P

DK = 64
EPS = 1e-06
MASKED = -1e30
BF = jnp.bfloat16
F32 = jnp.float32
MESH = pl.DeviceIdType.MESH
VMEM = pl.BlockSpec(memory_space=pltpu.VMEM)
ANY = pl.BlockSpec(memory_space=pl.ANY)
LIMIT = 510 * 128 * 1024
STEP = 256
SPACE = 2
PIECE = 32
TOK0 = 2
TOKR = 1
CORE0 = 4
CORE1 = 13


def dot(a, b):
    return jnp.dot(a, b, preferred_element_type=F32)


def dot_nt(a, b):
    return lax.dot_general(a, b, (((1,), (1,)), ((), ())), preferred_element_type=F32)


def dot_tn(a, b):
    return lax.dot_general(a, b, (((0,), (0,)), ((), ())), preferred_element_type=F32)


def norm_scale(x):
    return lax.rsqrt(jnp.mean(x * x, axis=-1, keepdims=True) + EPS)


def norm_back(x, r, g, u):
    w = u * g
    inner = jnp.mean(w * x, axis=-1, keepdims=True)
    return r * w - x * (r * r * r * inner), jnp.sum(u * (x * r), axis=0, keepdims=True)


def flip(index, bit):
    size = 1 << bit
    return index + size - 2 * size * lax.rem(index // size, 2)


def flip_all(index, mask):
    bit = 0
    while mask:
        if mask & 1:
            index = flip(index, bit)
        mask >>= 1
        bit += 1
    return index


def subsets(bits):
    out = [0]
    for b in bits:
        out = out + [m | (1 << b) for m in out]
    return out


def bit_orders(count):
    upper = list(range(1, count))
    return [upper + [0], upper[::-1] + [0]]


class Sems:
    def __init__(self, ref):
        self.ref = ref
        self.used = 0

    def take(self):
        self.used += 1
        return self.ref.at[self.used - 1]

    def many(self, count):
        base = self.used
        self.used += count
        return lambda n: self.ref.at[base + n]


def wait_bytes(ref, sem):
    pltpu.make_async_copy(ref, ref, sem).wait()


def row_loop(shape, body):
    size = 32 if shape[1] <= 256 else 16
    if shape[0] % size:
        body(slice(0, shape[0]))
        return

    def step(n, carry):
        body(pl.ds(pl.multiple_of(n * size, size), size))
        return carry

    lax.fori_loop(0, shape[0] // size, step, 0)


def add_into(ref, got):
    if len(ref.shape) == 2:

        def body(at):
            ref[at, :] = ref[at, :] + got[at, :]

        row_loop(ref.shape, body)
    else:

        def step(t, carry):
            ref[t] = ref[t] + got[t]
            return carry

        lax.fori_loop(0, ref.shape[0], step, 0)


def enter(nt, nd, all_tensor=False):
    me_t, me_d = lax.axis_index("tensor"), lax.axis_index("dp")
    bar = pltpu.get_barrier_semaphore()
    bits = nd.bit_length() - 1
    for b in range(bits):
        pl.semaphore_signal(bar, 1, device_id={"dp": flip(me_d, b)}, device_id_type=MESH)
    if all_tensor:
        for k in range(1, nt):
            pl.semaphore_signal(bar, 1, device_id={"tensor": lax.rem(me_t + k, nt)}, device_id_type=MESH)
        pl.semaphore_wait(bar, bits + nt - 1)
        return me_t, me_d

    @pl.when(me_t > 0)
    def _():
        pl.semaphore_signal(bar, 1, device_id={"tensor": me_t - 1}, device_id_type=MESH)

    @pl.when(me_t < nt - 1)
    def _():
        pl.semaphore_signal(bar, 1, device_id={"tensor": me_t + 1}, device_id_type=MESH)

    pl.semaphore_wait(bar, bits + (me_t + nt - 1) // nt + (2 * nt - 2 - me_t) // nt)
    return me_t, me_d


def run_jobs(jobs, after):
    events = []
    for number, (start, stages, ticks) in enumerate(jobs):
        for tick, stage in zip(ticks, stages, strict=True):
            events.append((start + tick, start, number, stage))
    for event in sorted(events, key=lambda e: e[:3]):
        event[3]()
    for fn in after:
        fn()


def line_gather(nt, me, own, slot, sends, recvs, after):
    sem = {(s, j): (sends.take(), recvs.take()) for s in (1, -1) for j in range(1, nt)}

    def send(side, j):
        block = me - side * (j - 1)
        target = me + side
        ok = (block >= 0) & (block < nt) & (target >= 0) & (target < nt)
        src = own if j == 1 else slot(jnp.clip(block, 0, nt - 1))
        dst = slot(jnp.clip(block, 0, nt - 1))
        ss, rs = sem[side, j]

        @pl.when(ok)
        def _():
            pltpu.make_async_remote_copy(
                src, dst, ss, rs, device_id={"tensor": target}, device_id_type=MESH
            ).start()

        def done():
            @pl.when(ok)
            def _():
                wait_bytes(own, ss)

        after.append(done)

    def arrive(side, j):
        block = me - side * j

        @pl.when((block >= 0) & (block < nt))
        def _():
            wait_bytes(own, sem[side, j][1])

    def stage(j):
        def run():
            for side in (1, -1):
                if j > 0:
                    arrive(side, j)
                if j < nt - 1:
                    send(side, j + 1)

        return run

    return [stage(j) for j in range(nt)]


def cube_gather(nd, me, order, own, slot, slots, sends, recvs, after):
    count = len(order)
    sem = [(sends.take(), recvs.take()) for _ in range(count)]

    def start(k):
        bit = order[k]
        for m in subsets(order[:k]):
            block = flip_all(me, m)
            src = own if (m == 0 and own is not None) else slot(block)
            pltpu.make_async_remote_copy(
                src, slot(block), sem[k][0], sem[k][1], device_id={"dp": flip(me, bit)}, device_id_type=MESH
            ).start()

        def done():
            wait_bytes(slots(1 << k), sem[k][0])

        after.append(done)

    def stage(k):
        def run():
            if k > 0:
                wait_bytes(slots(1 << (k - 1)), sem[k - 1][1])
            if k < count:
                start(k)

        return run

    return [stage(k) for k in range(count + 1)]


def forward_kernel(
    nt,
    nd,
    heads,
    tok_ref,
    enc_ref,
    wa_ref,
    wb_ref,
    segr_ref,
    bl_ref,
    tab_ref,
    tok_out,
    enc_out,
    wb_out,
    wa_full,
    gain_ref,
    qkv_ref,
    lse_ref,
    attn_ref,
    mine_ref,
    wa_out,
    strip,
    bias,
    qs,
    ks,
    vs,
    os,
    lses,
    ssem,
    rsem,
    lsem,
):
    me_t, me_d = enter(nt, nd, True)
    bits = nd.bit_length() - 1
    sends, recvs, after = Sems(ssem), Sems(rsem), []
    locals_ = [
        (tok_ref, tok_out.at[me_t]),
        (enc_ref, enc_out.at[me_t]),
        (wa_ref, wa_out.at[me_d]),
        (wb_ref, wb_out.at[me_t, me_d]),
    ]
    for n, (src, dst) in enumerate(locals_):
        pltpu.make_async_copy(src, dst, lsem.at[n]).start()
    orders = bit_orders(bits)
    cols = wb_ref.shape[1]
    chunks = cols // STEP
    half = STEP // 2
    jobs = []
    jobs.append(
        (
            0,
            cube_gather(nd, me_d, orders[0], wa_ref, lambda d: wa_out.at[d], lambda n: wa_out.at[pl.ds(0, n)], sends, recvs, after),
            [SPACE * k for k in range(bits + 1)],
        )
    )

    def chunk_job(c):
        first = c * STEP
        z = line_gather(
            nt,
            me_t,
            wb_ref.at[:, pl.ds(first, STEP)],
            lambda t: wb_out.at[t, me_d, :, pl.ds(first, STEP)],
            sends,
            recvs,
            after,
        )
        cubes = []
        for n in range(2):
            at = first + n * half
            cubes.append(
                cube_gather(
                    nd,
                    me_d,
                    orders[n],
                    None,
                    lambda d, at=at: wb_out.at[:, d, :, pl.ds(at, half)],
                    lambda k, at=at: wb_out.at[:, pl.ds(0, k), :, pl.ds(at, half)],
                    sends,
                    recvs,
                    after,
                )
            )

        def meet():
            z[-1]()
            for q in cubes:
                q[0]()

        def both(k):
            def run():
                for q in cubes:
                    q[k]()

            return run

        return z[:-1] + [meet] + [both(k) for k in range(1, bits + 1)]


    def row_job(ref, out, n):
        at = pl.ds(n * PIECE, PIECE)
        return line_gather(nt, me_t, ref.at[at], lambda t: out.at[t, at], sends, recvs, after)

    ticks = list(range(nt)) + [nt - 1 + SPACE * k for k in range(1, bits + 1)]
    for c in range(chunks):
        jobs.append((c, chunk_job(c), ticks))
    number = TOK0
    for ref, out in ((tok_ref, tok_out), (enc_ref, enc_out)):
        for n in range(ref.shape[0] // PIECE):
            jobs.append((number // TOKR, row_job(ref, out, n), list(range(nt))))
            number += 1
    pltpu.make_async_copy(wb_ref, wb_out.at[me_t, me_d], lsem.at[3]).wait()
    after.append(lambda: pltpu.make_async_copy(enc_ref, enc_out.at[me_t], lsem.at[1]).wait())

    block = tok_ref.shape[0]
    part = wa_ref.shape[0]
    hw = heads * DK
    bias[...] = bias_lines(bl_ref, tab_ref)[0]

    def rows_of(i):
        return slice(i * block, (i + 1) * block)

    def weights():
        for n in (0, 2):
            src, dst = locals_[n]
            pltpu.make_async_copy(src, dst, lsem.at[n]).wait()
        for d in range(nd):
            wa_full[d * part : (d + 1) * part, :] = wa_out[d]
        gain_ref[...] = wa_full[:, 3 * hw :].astype(F32).T[0:8]

    def rows_start(i):
        x = tok_out[i].astype(F32)
        n = (x * norm_scale(x) * gain_ref[0:1, :]).astype(BF)
        y = dot(n, wa_full[:, : 3 * hw]).astype(BF)
        qkv_ref[i] = y
        for h in range(heads):
            for which, ref in enumerate((qs, ks, vs)):
                at = which * hw + h * DK
                ref[h, rows_of(i), :] = y[:, at : at + DK]

    def head(h, carry):
        build_strip(strip, bias[pl.ds(h, 1), :])
        for i in range(nt):
            piece(h, i)
        return carry

    def piece(h, i):
        mine = rows_of(i)
        seen = (i + 1) * block
        off = (nt - 1 - i) * block
        s = dot_nt(qs[h, mine, :], ks[h, :seen, :])
        s = s + strip[:, off : off + seen]
        s = jnp.where(column(segr_ref[:, mine]) == segr_ref[:, :seen], s, MASKED)
        top = jnp.max(s, axis=-1, keepdims=True)
        p = jnp.exp(s - top)
        total = jnp.sum(p, axis=-1, keepdims=True)
        os[h, mine, :] = (dot(p.astype(BF), vs[h, :seen, :]) / total).astype(BF)
        lses[h, mine, :] = top + jnp.log(total)

    def collect():
        for i in range(nt):
            for h in range(heads):
                attn_ref[i, :, h * DK : (h + 1) * DK] = os[h, rows_of(i), :]
                lse_ref[rows_of(i), h : h + 1] = lses[h, rows_of(i), :]

    own = pltpu.make_async_copy(attn_ref.at[me_t], mine_ref.at[me_t], lsem.at[4])
    swaps = []
    for k in range(1, nt):
        peer = lax.rem(me_t + k, nt)
        swaps.append(
            pltpu.make_async_remote_copy(
                attn_ref.at[peer],
                mine_ref.at[me_t],
                sends.take(),
                recvs.take(),
                device_id={"tensor": peer},
                device_id_type=MESH,
            )
        )

    def swap():
        for copy in swaps + [own]:
            copy.start()

    after.extend(copy.wait for copy in swaps + [own])
    compute = [(CORE1, weights)] + [(CORE1, partial(rows_start, i)) for i in range(nt)]
    compute.append((CORE1 + 1, lambda: lax.fori_loop(0, heads, head, 0)))
    compute += [(CORE1 + 1, collect), (CORE1 + 1, swap)]
    for tick, fn in compute:
        jobs.append((tick, [fn], [0]))
    run_jobs(jobs, after)


def forward_all(nt, nd, heads, tok, enc, wa, wb, segr, bl, tab):
    bits = nd.bit_length() - 1
    chunks = wb.shape[1] // STEP
    lines = chunks + (tok.shape[0] + enc.shape[0]) // PIECE
    total = lines * 2 * (nt - 1) + (2 * chunks + 1) * bits + nt - 1
    block, width = tok.shape
    length = nt * block
    hw = heads * DK
    return pl.pallas_call(
        partial(forward_kernel, nt, nd, heads),
        out_shape=(
            jax.ShapeDtypeStruct((nt,) + tok.shape, BF),
            jax.ShapeDtypeStruct((nt,) + enc.shape, BF),
            jax.ShapeDtypeStruct((nt, nd) + wb.shape, BF),
            jax.ShapeDtypeStruct((width, wa.shape[1]), BF),
            jax.ShapeDtypeStruct((8, width), F32),
            jax.ShapeDtypeStruct((nt, block, 3 * hw), BF),
            jax.ShapeDtypeStruct((length, 8), F32),
            jax.ShapeDtypeStruct((nt, block, hw), BF),
            jax.ShapeDtypeStruct((nt, block, hw), BF),
        ),
        in_specs=[VMEM] * 7,
        out_specs=(VMEM, ANY, ANY) + (VMEM,) * 6,
        scratch_shapes=[
            pltpu.VMEM((nd,) + wa.shape, BF),
            pltpu.VMEM((block, length + block), F32),
            pltpu.VMEM((8, length + block), F32),
        ]
        + [pltpu.VMEM((heads, length, DK), BF)] * 4
        + [
            pltpu.VMEM((heads, length, 1), F32),
            pltpu.SemaphoreType.DMA((total,)),
            pltpu.SemaphoreType.DMA((total,)),
            pltpu.SemaphoreType.DMA((5,)),
        ],
        compiler_params=pltpu.CompilerParams(collective_id=0, has_side_effects=True, vmem_limit_bytes=LIMIT),
        name="forward_all",
    )(tok, enc, wa, wb, segr, bl, tab)


def cube_scatter(nd, me, order, value, recv, sends, recvs, after):
    count = len(order)
    sem = [(sends.take(), recvs.take()) for _ in range(count)]

    def start(k):
        bit = order[k]
        peer = flip(me, bit)
        for j, m in enumerate(subsets(order[k + 1 :])):
            pltpu.make_async_remote_copy(
                value(flip_all(peer, m)),
                recv[k].at[j],
                sem[k][0],
                sem[k][1],
                device_id={"dp": peer},
                device_id_type=MESH,
            ).start()

        def done():
            wait_bytes(recv[k], sem[k][0])

        after.append(done)

    def land(k):
        wait_bytes(recv[k], sem[k][1])
        for j, m in enumerate(subsets(order[k + 1 :])):
            add_into(value(flip_all(me, m)), recv[k].at[j])

    def stage(k):
        def run():
            if k > 0:
                land(k - 1)
            if k < count:
                start(k)

        return run

    return [stage(k) for k in range(count + 1)]


def line_scatter(nt, me, value, recv, out, sends, recvs, after):
    ssem, rsem = sends.many(2 * nt), recvs.many(2 * nt)

    def land(side, b):
        return recv.at[b + 1 - side]

    def hop(z):
        def run():
            for side, here in ((0, z), (1, nt - 1 - z)):
                goal = here + 1 if side == 0 else here - 1
                blocks = range(here + 1, nt) if side == 0 else range(here - 1, -1, -1)

                @pl.when(me == here)
                def _(side=side, goal=goal, blocks=blocks):
                    for b in blocks:
                        ref = value(b)
                        if z > 0:
                            got = land(side, b)
                            wait_bytes(got, rsem(side * nt + b))
                            add_into(ref, got)
                        pltpu.make_async_remote_copy(
                            ref,
                            land(side, b),
                            ssem(side * nt + b),
                            rsem(side * nt + b),
                            device_id={"tensor": goal},
                            device_id_type=MESH,
                        ).start()

        return run

    def last():
        own = value(me)

        def first(at):
            out[at, :] = own[at, :].astype(F32)

        row_loop(out.shape, first)
        for side, some in ((0, me > 0), (1, me < nt - 1)):

            @pl.when(some)
            def _(side=side):
                got = land(side, me)
                wait_bytes(got, rsem(side * nt + me))

                def more(at):
                    out[at, :] = out[at, :] + got[at, :].astype(F32)

                row_loop(out.shape, more)

    def done():
        for here in range(nt):

            @pl.when(me == here)
            def _(here=here):
                for b in range(here + 1, nt):
                    wait_bytes(land(0, b), ssem(b))
                for b in range(here):
                    wait_bytes(land(1, b), ssem(nt + b))

    after.append(done)
    return [hop(z) for z in range(nt - 1)] + [last]


def backward_kernel(
    nt,
    nd,
    heads,
    g_used,
    g_ref,
    e_ref,
    gain_in,
    dmine_ref,
    tok_ref,
    wa_ref,
    g0_ref,
    segr_ref,
    bl_ref,
    tab_ref,
    qkv_ref,
    lse_ref,
    g_out,
    a_out,
    u_out,
    e_out,
    *scratch,
):
    bits = nd.bit_length() - 1
    gv, uz, ez, gz = scratch[:4]
    arecv = scratch[4 : 4 + bits]
    grecv = scratch[4 + bits : 4 + 2 * bits]
    a_ref, u_ref, da_ref, strips, qs, ks, vs, das, dkt, dvt, dqkv, lines, bias, gain0 = scratch[4 + 2 * bits : 18 + 2 * bits]
    ssem, rsem, lsem = scratch[18 + 2 * bits :]
    cols = g_ref.shape[3]
    chunks = cols // STEP
    half = STEP // 2
    block = tok_ref.shape[1]
    hw = heads * DK
    width = strips.shape[1]
    strip, dstrip = strips.at[pl.ds(0, block)], strips.at[pl.ds(block, block)]
    gat = strips.at[pl.ds(0, 3 * hw), pl.ds(0, tok_ref.shape[2])]
    for c in range(chunks):
        at = pl.ds(c * STEP, STEP)
        pltpu.make_async_copy(g_ref.at[:, :, :, at], gv.at[:, :, :, at], lsem.at[c]).start()
    me_t, me_d = enter(nt, nd, True)
    sends, recvs, after = Sems(ssem), Sems(rsem), []
    orders = [[0] + o[:-1][::-1] for o in bit_orders(bits)]
    jobs = []

    own = pltpu.make_async_copy(dmine_ref.at[me_t], da_ref.at[me_t], lsem.at[chunks])
    own.start()
    swaps = []
    for k in range(1, nt):
        peer = lax.rem(me_t + k, nt)
        copy = pltpu.make_async_remote_copy(
            dmine_ref.at[peer], da_ref.at[me_t], sends.take(), recvs.take(), device_id={"tensor": peer}, device_id_type=MESH
        )
        copy.start()
        swaps.append(copy)

    def swapped():
        own.wait()
        for copy in swaps:
            copy.wait_recv()

    after.extend(copy.wait_send for copy in swaps)

    line, hot = bias_lines(bl_ref, tab_ref)

    def rows_of(i):
        return slice(i * block, (i + 1) * block)

    bias[...] = line

    def piece(h, i):
        mine = rows_of(i)
        seen = (i + 1) * block
        off = (nt - 1 - i) * block
        q = qs[mine, :]
        da = das[mine, :]
        s = dot_nt(q, ks[:seen, :])
        s = s + strip[:, off : off + seen]
        s = jnp.where(column(segr_ref[:, mine]) == segr_ref[:, :seen], s, MASKED)
        at = lax.broadcasted_iota(jnp.int32, (block, lse_ref.shape[1]), 1) == h
        lse = jnp.sum(jnp.where(at, lse_ref[mine, :], 0.0), axis=1, keepdims=True)
        p = jnp.exp(s - lse)
        dp = dot_nt(da, vs[:seen, :])
        ds = p * (dp - jnp.sum(p * dp, axis=1, keepdims=True))
        low = ds.astype(BF)
        dkt[:, :seen] += dot_tn(q, low)
        dvt[:, :seen] += dot_tn(da, p.astype(BF))
        dstrip[:, off : off + seen] += ds
        qs[mine, :] = dot(low, ks[:seen, :]).astype(BF)

    def head(h, carry):
        build_strip(strip, bias[pl.ds(h, 1), :])
        for k in range(heads):

            @pl.when(h == k)
            def _(k=k):
                for i in range(nt):
                    for which, ref in enumerate((qs, ks, vs)):
                        at = which * hw + k * DK
                        ref[rows_of(i), :] = qkv_ref[i, :, at : at + DK]
                    das[rows_of(i), :] = da_ref[i, :, k * DK : (k + 1) * DK]

        dstrip[...] = jnp.zeros_like(dstrip)
        dkt[...] = jnp.zeros_like(dkt)
        dvt[...] = jnp.zeros_like(dvt)
        for i in range(nt):
            piece(h, i)
        for i in range(nt):
            ks[rows_of(i), :] = dkt[:, rows_of(i)].T.astype(BF)
            vs[rows_of(i), :] = dvt[:, rows_of(i)].T.astype(BF)
        for k in range(heads):

            @pl.when(h == k)
            def _(k=k):
                for which, ref in enumerate((qs, ks, vs)):
                    at = which * hw + k * DK
                    dqkv[:, at : at + DK] = ref[...]

        n = block // 2
        while n >= 8:
            dstrip[0:n, :] = dstrip[0:n, :] + pltpu.roll(dstrip[n : 2 * n, :], width - n, 1)
            n //= 2
        x = dstrip[0:8, :]
        row = lax.broadcasted_iota(jnp.int32, x.shape, 0)
        for b in range(3):
            x = jnp.where((row >> b) % 2 == 1, pltpu.roll(x, width - (1 << b), 1), x)
        lines[pl.ds(h, 1), :] = jnp.sum(x, axis=0, keepdims=True)
        return carry

    def rows_end(i):
        mine = rows_of(i)
        x = tok_ref[i].astype(F32)
        hat = x * norm_scale(x)
        more = dot_tn(dqkv[mine, :], (hat * g0_ref[...]).astype(BF))
        gat[...] = more if i == 0 else gat[...] + more
        u = dot_nt(dqkv[mine, :], wa_ref[:, : 3 * hw])
        gain0[...] += jnp.sum(u * hat, axis=0, keepdims=True)
        u_ref[i] = u.astype(BF)

    def finish():
        table = lax.dot_general(
            lines[...],
            hot.astype(F32),
            (((1,), (1,)), ((), ())),
            precision=lax.Precision.HIGHEST,
            preferred_element_type=F32,
        )
        table = jnp.concatenate([table, jnp.zeros((8, 128 - table.shape[1]), F32)], axis=1).astype(BF)
        ga = gat[...].T.astype(BF)
        part = ga.shape[0] // nd
        for d in range(nd):
            a_ref[d, :, : 3 * hw] = ga[d * part : (d + 1) * part]
            a_ref[d, :, 3 * hw :] = jnp.zeros((part, 128), BF)
            a_ref[d, :8, 3 * hw :] = table

    def add_gains():
        at = g_used - (cols - 128)
        row = lax.broadcasted_iota(jnp.int32, (128, gain0.shape[1]), 0)
        gains = jnp.where(row == at, gain0[...], 0.0)
        gains = gains + jnp.where(row == at + 1, gain_in[0:1, :], 0.0) + jnp.where(row == at + 2, gain_in[1:2, :], 0.0)
        gains = gains.T.astype(BF)
        part = gains.shape[0] // nd

        def step(t, carry):
            for d in range(nd):
                gv[t, d, :, cols - 128 :] = gv[t, d, :, cols - 128 :] + gains[d * part : (d + 1) * part]
            return carry

        lax.fori_loop(0, nt, step, 0)

    lines[...] = jnp.zeros_like(lines)
    gain0[...] = jnp.zeros_like(gain0)

    def a_done():
        a_out[...] = a_ref[me_d].astype(F32)

    def chunk_job(c):
        first = c * STEP
        cubes = []
        for n in range(2):
            at = first + n * half
            cubes.append(
                cube_scatter(
                    nd,
                    me_d,
                    orders[n],
                    lambda d, at=at: gv.at[:, d, :, pl.ds(at, half)],
                    [r.at[2 * c + n] for r in grecv],
                    sends,
                    recvs,
                    after,
                )
            )
        z = line_scatter(
            nt,
            me_t,
            lambda b: gv.at[b, me_d, :, pl.ds(first, STEP)],
            gz.at[c],
            g_out.at[:, pl.ds(first, STEP)],
            sends,
            recvs,
            after,
        )

        def begin():
            at = pl.ds(first, STEP)
            pltpu.make_async_copy(g_ref.at[:, :, :, at], gv.at[:, :, :, at], lsem.at[c]).wait()
            if c == chunks - 1:
                add_gains()
            for q in cubes:
                q[0]()

        def both(k):
            def run():
                for q in cubes:
                    q[k]()

            return run

        def meet():
            for q in cubes:
                q[bits]()
            z[0]()

        return [begin] + [both(k) for k in range(1, bits)] + [meet] + z[1:]

    def row_job(ref, recv, out, n):
        at = pl.ds(n * PIECE, PIECE)
        return line_scatter(nt, me_t, lambda b: ref.at[b, at], recv.at[:, at], out.at[at], sends, recvs, after)

    ticks = [SPACE * k for k in range(bits)] + [SPACE * bits + k for k in range(nt)]
    for c in range(chunks):
        jobs.append((min(c, chunks - 1), chunk_job(c), ticks))
    for n in range(e_out.shape[0] // PIECE):
        jobs.append((n, row_job(e_ref, ez, e_out, n), list(range(nt))))
    compute = [(CORE0, swapped), (CORE0, lambda: lax.fori_loop(0, heads, head, 0))]
    ready = CORE0 + 1
    compute += [(ready, partial(rows_end, i)) for i in range(nt)]
    compute.append((ready, finish))
    for tick, fn in compute:
        jobs.append((tick, [fn], [0]))
    a_job = cube_scatter(nd, me_d, orders[0], lambda d: a_ref.at[d], arecv, sends, recvs, after) + [a_done]
    jobs.append((ready + 1, a_job, [SPACE * k for k in range(bits + 1)] + [SPACE * bits]))
    for n in range(u_out.shape[0] // PIECE):
        jobs.append((ready + 1 + n, row_job(u_ref, uz, u_out, n), list(range(nt))))
    run_jobs(jobs, after)


def backward_all(nt, nd, heads, used, g, e, gain12, dmine, tok, wa, g0, segr, bl, tab, qkv, lse):
    bits = nd.bit_length() - 1
    rows, cols = g.shape[2:]
    block, width = tok.shape[1:]
    length = nt * block
    wide = wa.shape[1]
    hw = heads * DK
    chunks = cols // STEP
    lines = chunks + (block + e.shape[1]) // PIECE
    total = lines * 2 * nt + (2 * chunks + 1) * bits + nt - 1
    return pl.pallas_call(
        partial(backward_kernel, nt, nd, heads, used),
        out_shape=(
            jax.ShapeDtypeStruct((rows, cols), F32),
            jax.ShapeDtypeStruct((rows, wide), F32),
            jax.ShapeDtypeStruct((block, width), F32),
            jax.ShapeDtypeStruct(e.shape[1:], F32),
        ),
        in_specs=[ANY] + [VMEM] * 11,
        out_specs=(VMEM,) * 4,
        scratch_shapes=[
            pltpu.VMEM((nt, nd, rows, cols), BF),
            pltpu.VMEM((nt + 1, block, width), BF),
            pltpu.VMEM((nt + 1,) + e.shape[1:], BF),
            pltpu.VMEM((chunks, nt + 1, rows, STEP), BF),
        ]
        + [pltpu.VMEM((1 << (bits - 1 - k), rows, wide), BF) for k in range(bits)]
        + [pltpu.VMEM((2 * chunks, 1 << (bits - 1 - k), nt, rows, STEP // 2), BF) for k in range(bits)]
        + [
            pltpu.VMEM((nd, rows, wide), BF),
            pltpu.VMEM((nt, block, width), BF),
            pltpu.VMEM((nt, block, hw), BF),
            pltpu.VMEM((max(2 * block, 3 * hw), length + block), F32),
            pltpu.VMEM((length, DK), BF),
            pltpu.VMEM((length, DK), BF),
            pltpu.VMEM((length, DK), BF),
            pltpu.VMEM((length, DK), BF),
            pltpu.VMEM((DK, length), F32),
            pltpu.VMEM((DK, length), F32),
            pltpu.VMEM((length, 3 * hw), BF),
            pltpu.VMEM((8, length + block), F32),
            pltpu.VMEM((8, length + block), F32),
            pltpu.VMEM((1, width), F32),
            pltpu.SemaphoreType.DMA((total,)),
            pltpu.SemaphoreType.DMA((total,)),
            pltpu.SemaphoreType.DMA((chunks + 1,)),
        ],
        compiler_params=pltpu.CompilerParams(collective_id=1, has_side_effects=True, vmem_limit_bytes=LIMIT),
        name="backward_all",
    )(g, e, gain12, dmine, tok, wa, g0, segr, bl, tab, qkv, lse)


def column(row):
    return jnp.broadcast_to(row, (8, row.shape[1])).T[:, 0:1]


def build_strip(strip, x):
    block, width = strip.shape
    row = lax.broadcasted_iota(jnp.int32, (8, width), 0)
    x = jnp.broadcast_to(x, (8, width))
    for b in range(3):
        x = jnp.where((row >> b) % 2 == 1, pltpu.roll(x, 1 << b, 1), x)
    strip[0:8, :] = x
    n = 8
    while n < block:
        strip[n : 2 * n, :] = pltpu.roll(strip[0:n, :], n, 1)
        n *= 2


def bias_lines(bl_ref, tab_ref):
    width = bl_ref.shape[1]
    buckets = tab_ref.shape[1]
    hot = bl_ref[...] == lax.broadcasted_iota(jnp.int32, (buckets, width), 0)
    line = dot(tab_ref[...], hot.astype(F32).astype(BF))
    return jnp.where(bl_ref[...] >= 0, line, MASKED), hot


def middle_kernel(
    heads,
    ff,
    tok_ref,
    enc_ref,
    attn_ref,
    og_ref,
    gains_ref,
    w_hbm,
    layer_ref,
    one_ref,
    denc_ref,
    gain_ref,
    dattn_ref,
    g_hbm,
    w,
    g,
    h1_ref,
    h2_ref,
    n1_ref,
    n2_ref,
    acc_ref,
    dn_ref,
    g2_ref,
    denc,
    qc,
    kv,
    ac,
    oc,
    lse,
    dkv,
    insem,
    outsem,
):
    nt = w.shape[0]
    hw = heads * DK
    cols = w.shape[2]
    f0, f1, f2 = 0, ff, 2 * ff
    kv0 = 3 * ff
    q0 = kv0 + 2 * hw
    c0 = q0 + hw
    s0 = c0 + hw
    end = s0 + hw
    ffn = pl.ds(0, 3 * ff)
    att = pl.ds(3 * ff, cols - 3 * ff)
    loads = [pltpu.make_async_copy(w_hbm.at[t, :, att], w.at[t, :, att], insem.at[0, t]) for t in range(nt)]
    loads += [pltpu.make_async_copy(w_hbm.at[t, :, ffn], w.at[t, :, ffn], insem.at[1, t]) for t in range(nt)]
    for copy in loads:
        copy.start()

    def load_wait(which, t):
        at = att if which == 0 else ffn
        pltpu.make_async_copy(w_hbm.at[t, :, at], w.at[t, :, at], insem.at[which, t]).wait()

    def store(which, t):
        at = att if which == 0 else ffn
        return pltpu.make_async_copy(g.at[t, :, at], g_hbm.at[t, :, at], outsem.at[which, t])

    acc_ref[...] = tok_ref[...].astype(F32)

    def self_out(t, carry):
        load_wait(0, t)
        acc_ref[...] += dot_nt(attn_ref[t], w[t, :, s0:end])
        return carry

    lax.fori_loop(0, nt, self_out, 0)
    h1 = acc_ref[...]
    h1_ref[...] = h1
    n1_ref[...] = (h1 * norm_scale(h1) * gains_ref[1:2, :]).astype(BF)

    def cross(t, carry):
        q = dot(n1_ref[...], w[t, :, q0:c0]).astype(BF)
        both = dot(enc_ref[...], w[t, :, kv0:q0]).astype(BF)
        qc[t] = q
        kv[t] = both
        outs = []
        for h in range(heads):
            part = slice(h * DK, (h + 1) * DK)
            s = dot_nt(q[:, part], both[:, part])
            top = jnp.max(s, axis=-1, keepdims=True)
            p = jnp.exp(s - top)
            total = jnp.sum(p, axis=-1, keepdims=True)
            lse[t, h] = top + jnp.log(total)
            outs.append(dot(p.astype(BF), both[:, hw + h * DK : hw + (h + 1) * DK]) / total)
        a = jnp.concatenate(outs, axis=1).astype(BF)
        ac[t] = a
        acc_ref[...] += dot_nt(a, w[t, :, c0:s0])
        return carry

    lax.fori_loop(0, nt, cross, 0)
    h2 = acc_ref[...]
    h2_ref[...] = h2
    n2_ref[...] = (h2 * norm_scale(h2) * gains_ref[2:3, :]).astype(BF)
    dn_ref[...] = jnp.zeros_like(dn_ref)

    def units(t, carry):
        load_wait(1, t)
        n2 = n2_ref[...]
        og = og_ref[...]
        gate = dot(n2, w[t, :, f0:f1])
        up = dot(n2, w[t, :, f1:f2])
        dinner = dot(og, w[t, :, f2 : 3 * ff])
        sq = gate * gate
        th = jnp.tanh(0.7978845608028654 * (gate + 0.044715 * (gate * sq)))
        cdf = 0.5 * (1.0 + th)
        act = gate * cdf
        slope = cdf + gate * (0.5 * (1.0 - th * th)) * (0.7978845608028654 * (1.0 + 0.134145 * sq))
        inner = (act * up).astype(BF)
        dgate = (dinner * up * slope).astype(BF)
        dup = (dinner * act).astype(BF)
        acc_ref[...] += dot_nt(inner, w[t, :, f2 : 3 * ff])
        dn_ref[...] += dot_nt(dgate, w[t, :, f0:f1]) + dot_nt(dup, w[t, :, f1:f2])
        g[t, :, f0:f1] = dot_tn(n2, dgate).astype(BF)
        g[t, :, f1:f2] = dot_tn(n2, dup).astype(BF)
        g[t, :, f2 : 3 * ff] = dot_tn(og, inner).astype(BF)
        store(1, t).start()
        return carry

    lax.fori_loop(0, nt, units, 0)
    layer_ref[...] = acc_ref[...].astype(BF)
    h2 = h2_ref[...]
    back, gain2 = norm_back(h2, norm_scale(h2), gains_ref[2:3, :], dn_ref[...])
    g2 = og_ref[...].astype(F32) + back
    acc_ref[...] = g2
    g2_ref[...] = g2.astype(BF)
    dn_ref[...] = jnp.zeros_like(dn_ref)
    denc[...] = jnp.zeros_like(denc)

    def cross_back(t, carry):
        g2 = g2_ref[...]
        a = ac[t]
        da = dot(g2, w[t, :, c0:s0]).astype(BF)
        g[t, :, c0:s0] = dot_tn(g2, a).astype(BF)
        prod = da.astype(F32) * a.astype(F32)
        q = qc[t]
        both = kv[t]
        dqs = []
        for h in range(heads):
            part = slice(h * DK, (h + 1) * DK)
            qh, kh = q[:, part], both[:, part]
            vh, dah = both[:, hw + h * DK : hw + (h + 1) * DK], da[:, part]
            p = jnp.exp(dot_nt(qh, kh) - lse[t, h])
            delta = jnp.sum(prod[:, part], axis=1, keepdims=True)
            ds = (p * (dot_nt(dah, vh) - delta)).astype(BF)
            dqs.append(dot(ds, kh))
            dkv[h * DK : (h + 1) * DK, :] = dot_tn(qh, ds)
            dkv[hw + h * DK : hw + (h + 1) * DK, :] = dot_tn(dah, p.astype(BF))
        dq = jnp.concatenate(dqs, axis=1).astype(BF)
        dboth = dkv[...].astype(BF)
        g[t, :, q0:c0] = dot_tn(n1_ref[...], dq).astype(BF)
        g[t, :, kv0:q0] = lax.dot_general(
            enc_ref[...], dboth, (((0,), (1,)), ((), ())), preferred_element_type=F32
        ).astype(BF)
        dn_ref[...] += dot_nt(dq, w[t, :, q0:c0])
        denc[...] += lax.dot_general(
            dboth, w[t, :, kv0:q0], (((0,), (1,)), ((), ())), preferred_element_type=F32
        )
        return carry

    lax.fori_loop(0, nt, cross_back, 0)
    denc_ref[...] = denc[...].astype(BF)
    h1 = h1_ref[...]
    back, gain1 = norm_back(h1, norm_scale(h1), gains_ref[1:2, :], dn_ref[...])
    g1 = acc_ref[...] + back
    one_ref[...] = g1
    g2_ref[...] = g1.astype(BF)
    gain_ref[...] = jnp.concatenate([gain1, gain2, jnp.zeros((6, gain1.shape[1]), F32)], axis=0)

    def self_out_back(t, carry):
        low = g2_ref[...]
        dattn_ref[t] = dot(low, w[t, :, s0:end]).astype(BF)
        tail = dot_tn(low, attn_ref[t])
        g[t, :, s0:cols] = jnp.concatenate([tail, jnp.zeros((tail.shape[0], cols - end), F32)], axis=1).astype(BF)
        store(0, t).start()
        return carry

    lax.fori_loop(0, nt, self_out_back, 0)
    for t in range(nt):
        store(1, t).wait()
        store(0, t).wait()


def middle(heads, ff, tok, enc, attn, og, gains, w):
    nt, _, cols = w.shape
    rows, width = tok.shape
    states = enc.shape[0]
    hw = heads * DK
    return pl.pallas_call(
        partial(middle_kernel, heads, ff),
        out_shape=(
            jax.ShapeDtypeStruct((rows, width), BF),
            jax.ShapeDtypeStruct((rows, width), F32),
            jax.ShapeDtypeStruct((states, width), BF),
            jax.ShapeDtypeStruct((8, width), F32),
            jax.ShapeDtypeStruct((nt, rows, hw), BF),
            jax.ShapeDtypeStruct(w.shape, BF),
        ),
        in_specs=[VMEM] * 5 + [ANY],
        out_specs=(VMEM,) * 5 + (ANY,),
        scratch_shapes=[
            pltpu.VMEM(w.shape, BF),
            pltpu.VMEM(w.shape, BF),
            pltpu.VMEM((rows, width), F32),
            pltpu.VMEM((rows, width), F32),
            pltpu.VMEM((rows, width), BF),
            pltpu.VMEM((rows, width), BF),
            pltpu.VMEM((rows, width), F32),
            pltpu.VMEM((rows, width), F32),
            pltpu.VMEM((rows, width), BF),
            pltpu.VMEM((states, width), F32),
            pltpu.VMEM((nt, rows, hw), BF),
            pltpu.VMEM((nt, states, 2 * hw), BF),
            pltpu.VMEM((nt, rows, hw), BF),
            pltpu.VMEM((8, 128), F32),
            pltpu.VMEM((nt, heads, rows, 1), F32),
            pltpu.VMEM((2 * hw, states), F32),
            pltpu.SemaphoreType.DMA((2, nt)),
            pltpu.SemaphoreType.DMA((2, nt)),
        ],
        compiler_params=pltpu.CompilerParams(vmem_limit_bytes=LIMIT),
        name="middle",
    )(tok, enc, attn, og, gains, w)


def per_device(
    tokens,
    encoder,
    segments,
    rel_bucket,
    out_grad,
    self_q,
    self_k,
    self_v,
    self_o,
    cross_q,
    cross_k,
    cross_v,
    cross_o,
    ffn_gate,
    ffn_up,
    ffn_down,
    bias_table,
    norm_gains,
):
    nt, nd = lax.axis_size("tensor"), lax.axis_size("dp")
    part, hw = self_q.shape
    ff = ffn_gate.shape[1]
    heads = hw // DK
    rows, width = tokens.shape
    length = rows * nt
    buckets = bias_table.shape[0]
    wa = jnp.concatenate([self_q, self_k, self_v, jnp.pad(norm_gains.T, ((0, 0), (0, 128 - norm_gains.shape[0])))], axis=1)
    wb = jnp.concatenate([ffn_gate, ffn_up, ffn_down.T, cross_k, cross_v, cross_q, cross_o.T, self_o.T], axis=1)
    used = wb.shape[1]
    cols = -(-(used + 3) // STEP) * STEP
    wb = jnp.pad(wb, ((0, 0), (0, cols - used)))
    top = (nt - 1) * rows
    blank = jnp.full((length - 1 - top,), -1, jnp.int32)
    bl = jnp.concatenate(
        [rel_bucket[: top + 1][::-1], blank, jnp.full((1,), -1, jnp.int32), rel_bucket[top + 1 : length][::-1]]
    )[None, :]
    tab = jnp.pad(bias_table.T, ((0, 8 - heads), (0, 0)))
    segr = segments
    tok_all, enc_all, wb_all, wa_full, gains, qkv, lse, attn, mine = forward_all(
        nt, nd, heads, tokens, encoder, wa, wb, segr, bl, tab
    )
    wb_full = wb_all.reshape(nt, nd * part, cols)
    g0 = gains[0:1]
    layer_out, grad_one, denc, gain12, dmine, gb = middle(
        heads, ff, tokens, enc_all.reshape(nt * encoder.shape[0], width), mine, out_grad, gains, wb_full
    )
    gsum, asum, usum, esum = backward_all(
        nt,
        nd,
        heads,
        used,
        gb.reshape(nt, nd, part, cols),
        denc.reshape((nt,) + encoder.shape),
        gain12,
        dmine,
        tok_all,
        wa_full,
        g0,
        segr,
        bl,
        tab,
        qkv,
        lse,
    )
    x = tokens.astype(F32)
    back, _ = norm_back(x, norm_scale(x), g0, usum)
    tokens_grad = grad_one + back
    at = 3 * ff
    ck, cv, cq, co, so = (gsum[:, at + n * hw : at + (n + 1) * hw] for n in range(5))
    return (
        layer_out,
        tokens_grad,
        esum,
        asum[:, :hw],
        asum[:, hw : 2 * hw],
        asum[:, 2 * hw : 3 * hw],
        so.T,
        cq,
        ck,
        cv,
        co.T,
        gsum[:, :ff],
        gsum[:, ff : 2 * ff],
        gsum[:, 2 * ff : 3 * ff].T,
        asum[:heads, 3 * hw : 3 * hw + buckets].T,
        gsum[:, used : used + 3].T,
    )


def solution(mesh):
    rows = P(("dp", "tensor"), None)
    left = P("dp", "tensor")
    right = P("tensor", "dp")
    return jax.shard_map(
        per_device,
        mesh=mesh,
        in_specs=(rows, rows, P("dp", None), P(), rows, left, left, left, right, left, left, left, right, left, left, right)
        + (P(None, "tensor"), P(None, "dp")),
        out_specs=(rows, rows, rows, left, left, left, right, left, left, left, right, left, left, right)
        + (P(None, "tensor"), P(None, "dp")),
        check_vma=False,
    )
```

profile of v0, /device:TPU:0, one launch (start us, length us, event | category | flops | bytes accessed | tf_op | source)
XLA Modules:
  0.0 280.6 jit_solution(10057736919070302653)
XLA Ops:
  0.6 0.0 copy-start.8
  0.7 0.0 copy-start.7
  0.7 0.0 copy-start.6
  0.7 0.0 copy-start.5
  0.7 0.8 reverse
  1.5 0.1 slice.70
  1.6 0.8 slice.49
  2.3 0.1 reverse.1
  2.4 0.1 slice.71
  2.5 0.1 concatenate.11
  2.6 0.6 broadcast_in_dim.9.bl_ref
  3.2 1.3 pad.14.tab_ref
  4.4 0.9 copy.35
  5.3 0.9 copy.36
  6.2 1.1 concatenate.10
  7.4 0.8 pad.13.wb_ref
  8.2 0.0 copy-done.8
  8.2 0.1 copy.34
  8.3 0.0 copy-done.7
  8.3 0.0 copy-done.6
  8.3 0.0 copy-done.5
  8.3 0.8 fusion.5.wa_ref
  9.1 102.9 %forward_all.1 = (bf16[4,256,768]{2,1,0:T(8,128)(2,1)}, bf16[4,128,768]{2,1,0:T(8,128)(2,1)}, bf16[4,8,96,2560]{3,2,1,0:T(8,128)(2,1)}, bf16[768,704]{1,0:T(8,12...) custom-call(bf16[256,768]{1,0:T(8,128)(2,1)} %tok_ref.3, ...), custom_call_target="tpu_custom_call" | custom-call | tf_op jit(solution)/shard_map/forward_all/pallas_call | solution.py:435
  112.0 39.3 %middle.1 = (bf16[256,768]{1,0:T(8,128)(2,1)}, f32[256,768]{1,0:T(8,128)}, bf16[512,768]{1,0:T(8,128)(2,1)}, f32[8,768]{1,0:T(8,128)}, bf16[4,256,192]{2,1,0:T(8,128)(2,1)}, /*index=5*/bf16[4,768,2560]{2,1,0:T(8,128)(2,1)}) custom-call(bf16[256,768]{1,0:T(8,128)(2,1)} %tok_ref.3, bf16[512,768]{1,0:T(8,128)(2,1)} %bitcast.25, ...), custom_call_target="tpu_custom_call" | custom-call | tf_op jit(solution)/shard_map/middle/pallas_call | solution.py:1082
  151.4 1.3 slice_reduce_fusion
  152.7 119.0 %backward_all.1 = (f32[96,2560]{1,0:T(8,128)}, f32[96,704]{1,0:T(8,128)}, f32[256,768]{1,0:T(8,128)}, f32[128,768]{1,0:T(8,128)}) custom-call(bf16[4,8,96,2560]{3,2,1,0:T(8,128)(2,1)} %bitcast.23, bf16[4,128,768]{2,1,0:T(8,128)(2,1)} %bitcast.24, f32[8,768]{1,0:T(8,128)} %get-tuple-element.42.gain_in, bf16[4,256,192]{2,1,0:T(8,128)(2,1)} %get-tuple-element.43.dmine_ref, ...), custom_call_target="tpu_custom_call" | custom-call | tf_op jit(solution)/shard_map/backward_all/pallas_call | solution.py:828
  271.7 0.0 copy-start
  271.7 0.0 copy-start.1
  271.7 0.0 copy-start.3
  271.7 2.3 slice_bitcast_fusion.1
  274.0 0.7 copy.37
  274.7 0.7 copy.38
  275.5 0.0 copy-done
  275.5 0.0 copy-done.1
  275.5 0.2 fusion
  275.7 0.0 copy-start.2
  275.7 0.0 copy-done.3
  275.7 0.0 copy-start.4
  275.7 1.1 fusion.3
  276.8 0.1 copy-done.2
  277.0 0.8 slice_bitcast_fusion
  277.8 0.1 slice_bitcast_fusion.3
  277.9 0.7 copy.39
  278.5 1.3 slice_bitcast_fusion.4
  279.9 0.0 copy-done.4
  279.9 0.7 copy.41
  (2 shorter events, 0.0 us)
Async XLA Ops:
  0.6 7.6 %copy-start.8 = (bf16[3,96]{1,0:T(4,128)(2,1)S(1)}, bf16[3,96]{1,0:T(4,128)(2,1)}, u32[]{:S(2)}) copy-start(bf16[3,96]{1,0:T(4,128)(2,1)} %param.35) | copy-start | bytes 1732
  0.7 7.7 %copy-start.7 = (bf16[96,192]{1,0:T(8,128)(2,1)S(1)}, bf16[96,192]{1,0:T(8,128)(2,1)}, u32[]{:S(2)}) copy-start(bf16[96,192]{1,0:T(8,128)(2,1)} %param.23) | copy-start | bytes 110596
  0.7 7.7 %copy-start.6 = (bf16[96,192]{1,0:T(8,128)(2,1)S(1)}, bf16[96,192]{1,0:T(8,128)(2,1)}, u32[]{:S(2)}) copy-start(bf16[96,192]{1,0:T(8,128)(2,1)} %param.24) | copy-start | bytes 110596
  0.7 7.7 %copy-start.5 = (bf16[96,192]{1,0:T(8,128)(2,1)S(1)}, bf16[96,192]{1,0:T(8,128)(2,1)}, u32[]{:S(2)}) copy-start(bf16[96,192]{1,0:T(8,128)(2,1)} %param.25) | copy-start | bytes 110596
  271.7 3.8 %copy-start = (bf16[256,768]{1,0:T(8,128)(2,1)S(1)}, bf16[256,768]{1,0:T(8,128)(2,1)}, u32[]{:S(2)}) copy-start(bf16[256,768]{1,0:T(8,128)(2,1)} %tok_ref.3) | copy-start | bytes 1179652
  271.7 3.8 %copy-start.1 = (f32[256,768]{1,0:T(8,128)S(1)}, f32[256,768]{1,0:T(8,128)}, u32[]{:S(2)}) copy-start(f32[256,768]{1,0:T(8,128)} %get-tuple-element.48) | copy-start | bytes 2359300
  271.7 4.0 %copy-start.3 = (f32[256,768]{1,0:T(8,128)S(1)}, f32[256,768]{1,0:T(8,128)}, u32[]{:S(2)}) copy-start(f32[256,768]{1,0:T(8,128)} %get-tuple-element.39) | copy-start | bytes 2359300
  275.7 1.3 copy-start.2
  275.7 4.1 %copy-start.4 = (f32[128,768]{1,0:T(8,128)S(1)}, f32[128,768]{1,0:T(8,128)}, u32[]{:S(2)}) copy-start(f32[128,768]{1,0:T(8,128)} %get-tuple-element.106) | copy-start | bytes 1179652
where the time goes:
time: 281 us
  Pallas kernels  261 us (93%)
  local copies, waits for them, and re-layouts  16.5 us (6%)
    pallas_call x1, Pallas kernels, backward_all(): pl.pallas_call(partial(backward_kernel, nt, nd, heads, used), out_shape=(...  119 us
    pallas_call x1, Pallas kernels, forward_all(): pl.pallas_call(partial(forward_kernel, nt, nd, heads), out_shape=(jax.Sha...  103 us
    pallas_call x1, Pallas kernels, middle(): pl.pallas_call(partial(middle_kernel, heads, ff), out_shape=(jax.ShapeDty...  39.3 us
    unnamed x29, local copies, waits for them, and re-layouts  6.02 us

commit v1 on v0

--- a/solution.py
+++ b/solution.py
@@ -21,7 +21,7 @@
 PIECE = 32
 TOK0 = 2
 TOKR = 1
-CORE0 = 4
+CORE0 = 3
 CORE1 = 13
 
 

time: 281 us -> 283 us (level)
  no operation moved by 1% of the time
where the time goes in v1:
time: 283 us
  Pallas kernels  263 us (93%)
  local copies, waits for them, and re-layouts  16.5 us (6%)
    pallas_call x1, Pallas kernels, backward_all(): pl.pallas_call(partial(backward_kernel, nt, nd, heads, used), out_shape=(...  121 us
    pallas_call x1, Pallas kernels, forward_all(): pl.pallas_call(partial(forward_kernel, nt, nd, heads), out_shape=(jax.Sha...  103 us
    pallas_call x1, Pallas kernels, middle(): pl.pallas_call(partial(middle_kernel, heads, ff), out_shape=(jax.ShapeDty...  39.3 us
    unnamed x29, local copies, waits for them, and re-layouts  6.02 us

profile of v1, /device:TPU:0, one launch (start us, length us, event | category | flops | bytes accessed | tf_op | source)
XLA Modules:
  0.0 282.8 jit_solution(8539321803938187733)
XLA Ops:
  0.6 0.0 copy-start.8
  0.7 0.0 copy-start.7
  0.7 0.0 copy-start.6
  0.7 0.0 copy-start.5
  0.7 0.8 reverse
  1.5 0.1 slice.70
  1.6 0.8 slice.49
  2.3 0.1 reverse.1
  2.4 0.1 slice.71
  2.5 0.1 concatenate.11
  2.6 0.6 broadcast_in_dim.9.bl_ref
  3.2 1.3 pad.14.tab_ref
  4.4 0.9 copy.35
  5.3 0.9 copy.36
  6.2 1.1 concatenate.10
  7.4 0.8 pad.13.wb_ref
  8.2 0.0 copy-done.8
  8.2 0.1 copy.34
  8.3 0.0 copy-done.7
  8.3 0.0 copy-done.6
  8.3 0.0 copy-done.5
  8.3 0.8 fusion.5.wa_ref
  9.1 102.9 %forward_all.1 = (bf16[4,256,768]{2,1,0:T(8,128)(2,1)}, bf16[4,128,768]{2,1,0:T(8,128)(2,1)}, bf16[4,8,96,2560]{3,2,1,0:T(8,128)(2,1)}, bf16[768,704]{1,0:T(8,12...) custom-call(bf16[256,768]{1,0:T(8,128)(2,1)} %tok_ref.3, ...), custom_call_target="tpu_custom_call" | custom-call | tf_op jit(solution)/shard_map/forward_all/pallas_call | solution.py:435
  112.0 39.3 %middle.1 = (bf16[256,768]{1,0:T(8,128)(2,1)}, f32[256,768]{1,0:T(8,128)}, bf16[512,768]{1,0:T(8,128)(2,1)}, f32[8,768]{1,0:T(8,128)}, bf16[4,256,192]{2,1,0:T(8,128)(2,1)}, /*index=5*/bf16[4,768,2560]{2,1,0:T(8,128)(2,1)}) custom-call(bf16[256,768]{1,0:T(8,128)(2,1)} %tok_ref.3, bf16[512,768]{1,0:T(8,128)(2,1)} %bitcast.25, ...), custom_call_target="tpu_custom_call" | custom-call | tf_op jit(solution)/shard_map/middle/pallas_call | solution.py:1082
  151.4 1.3 slice_reduce_fusion
  152.7 121.2 %backward_all.1 = (f32[96,2560]{1,0:T(8,128)}, f32[96,704]{1,0:T(8,128)}, f32[256,768]{1,0:T(8,128)}, f32[128,768]{1,0:T(8,128)}) custom-call(bf16[4,8,96,2560]{3,2,1,0:T(8,128)(2,1)} %bitcast.23, bf16[4,128,768]{2,1,0:T(8,128)(2,1)} %bitcast.24, f32[8,768]{1,0:T(8,128)} %get-tuple-element.42.gain_in, bf16[4,256,192]{2,1,0:T(8,128)(2,1)} %get-tuple-element.43.dmine_ref, ...), custom_call_target="tpu_custom_call" | custom-call | tf_op jit(solution)/shard_map/backward_all/pallas_call | solution.py:828
  273.9 0.0 copy-start
  273.9 0.0 copy-start.1
  273.9 0.0 copy-start.3
  273.9 2.3 slice_bitcast_fusion.1
  276.2 0.7 copy.37
  276.9 0.7 copy.38
  277.7 0.0 copy-done
  277.7 0.0 copy-done.1
  277.7 0.2 fusion
  277.9 0.0 copy-start.2
  277.9 0.0 copy-done.3
  278.0 0.0 copy-start.4
  278.0 1.1 fusion.3
  279.0 0.1 copy-done.2
  279.2 0.8 slice_bitcast_fusion
  280.0 0.1 slice_bitcast_fusion.3
  280.1 0.7 copy.39
  280.7 1.3 slice_bitcast_fusion.4
  282.1 0.0 copy-done.4
  282.1 0.7 copy.41
  (2 shorter events, 0.0 us)
Async XLA Ops:
  0.6 7.6 %copy-start.8 = (bf16[3,96]{1,0:T(4,128)(2,1)S(1)}, bf16[3,96]{1,0:T(4,128)(2,1)}, u32[]{:S(2)}) copy-start(bf16[3,96]{1,0:T(4,128)(2,1)} %param.35) | copy-start | bytes 1732
  0.7 7.7 %copy-start.7 = (bf16[96,192]{1,0:T(8,128)(2,1)S(1)}, bf16[96,192]{1,0:T(8,128)(2,1)}, u32[]{:S(2)}) copy-start(bf16[96,192]{1,0:T(8,128)(2,1)} %param.23) | copy-start | bytes 110596
  0.7 7.7 %copy-start.6 = (bf16[96,192]{1,0:T(8,128)(2,1)S(1)}, bf16[96,192]{1,0:T(8,128)(2,1)}, u32[]{:S(2)}) copy-start(bf16[96,192]{1,0:T(8,128)(2,1)} %param.24) | copy-start | bytes 110596
  0.7 7.7 %copy-start.5 = (bf16[96,192]{1,0:T(8,128)(2,1)S(1)}, bf16[96,192]{1,0:T(8,128)(2,1)}, u32[]{:S(2)}) copy-start(bf16[96,192]{1,0:T(8,128)(2,1)} %param.25) | copy-start | bytes 110596
  273.9 3.8 %copy-start = (bf16[256,768]{1,0:T(8,128)(2,1)S(1)}, bf16[256,768]{1,0:T(8,128)(2,1)}, u32[]{:S(2)}) copy-start(bf16[256,768]{1,0:T(8,128)(2,1)} %tok_ref.3) | copy-start | bytes 1179652
  273.9 3.8 %copy-start.1 = (f32[256,768]{1,0:T(8,128)S(1)}, f32[256,768]{1,0:T(8,128)}, u32[]{:S(2)}) copy-start(f32[256,768]{1,0:T(8,128)} %get-tuple-element.48) | copy-start | bytes 2359300
  273.9 4.0 %copy-start.3 = (f32[256,768]{1,0:T(8,128)S(1)}, f32[256,768]{1,0:T(8,128)}, u32[]{:S(2)}) copy-start(f32[256,768]{1,0:T(8,128)} %get-tuple-element.39) | copy-start | bytes 2359300
  277.9 1.3 copy-start.2
  278.0 4.1 %copy-start.4 = (f32[128,768]{1,0:T(8,128)S(1)}, f32[128,768]{1,0:T(8,128)}, u32[]{:S(2)}) copy-start(f32[128,768]{1,0:T(8,128)} %get-tuple-element.106) | copy-start | bytes 1179652
